TPU v7x, 32 devices: a whole 2x2x4 slice. The times are simulated.
32 devices in a mesh: rows: 4 (over y, core), cols: 8 (over z, x).
Axes of the slice: x: 2, y: 2, z: 4, core: 2. Of those that a mesh axis runs over, the one named last changes fastest.
Arguments:
- costs: bfloat16 [4, 8, 24, 256, 256], P('rows', 'cols'), may hold values from -210 to 8
- block_rows: int32 [4, 8, 24], P('rows', 'cols'), may hold values from 0 to 7, as said below
- block_cols: int32 [4, 8, 24], P('rows', 'cols'), may hold values from 0 to 63, as said below
- live: int32 [4, 8], P('rows', 'cols'), may hold values from 16 to 24, as said below
- log_source: float32 [8192], P('rows'), may hold values from -6 to 6
- log_target: float32 [131072], P('cols'), may hold values from -6 to 6
Outputs:
- source_potential: float32 [8192], P('rows')
- target_potential: float32 [131072], P('cols')
Inputs may be any that keep to these rules, and one draw needn't show every extreme that they name: `block_rows`: row blocks are local to a device's 8 blocks of source cells. `block_cols`: column blocks are local to a device's 64 blocks of target cells. Every source cell and every target cell lies in some live block. `live`: live counts differ from device to device; some device uses all 24 slots.
All inputs are finite; a program needn't handle non-finite values.
Results may differ from a plain program's by a relative error of at most 0.0003.
Values sent between devices are 32-bit elements; how exact they have to be, the bound alone decides.
A program may use at most 64 MiB of HBM per device.

v0:
```python
import jax
import jax.numpy as jnp
from jax import lax
from jax.sharding import PartitionSpec as P

ITERS = 3
NEG = -1e30


def combined_all(value, axis, combine):
    everything = jax.tree.map(lambda part: lax.all_gather(part, axis), value)
    first = jax.tree.map(lambda part: part[0], everything)

    def hop(k, so_far):
        return combine(so_far, jax.tree.map(lambda part: part[k], everything))

    return lax.fori_loop(1, lax.axis_size(axis), hop, first)


def combine(first, second):
    top_a, tot_a = first
    top_b, tot_b = second
    top = jnp.maximum(top_a, top_b)
    return (top, tot_a * jnp.exp(top_a - top) + tot_b * jnp.exp(top_b - top))


def block_reduce(slot_top, score_fn, blocks_of, blocks, valid):
    select = (blocks_of[:, None] == jnp.arange(blocks, dtype=jnp.int32)[None, :]) & valid[:, None]
    block_top = jnp.max(jnp.where(select[:, :, None], slot_top[:, None, :], NEG), axis=0)
    own_top = jnp.max(jnp.where(select[:, :, None], block_top[None, :, :], NEG), axis=1)
    own_top = jnp.where(valid[:, None], own_top, 0.0)
    sums = score_fn(own_top)
    sums = jnp.where(valid[:, None], sums, 0.0)
    total = jnp.sum(jnp.where(select[:, :, None], sums[:, None, :], 0.0), axis=0)
    return (block_top.reshape(-1), total.reshape(-1))


def row_partial(tiles, rows_blk, cols_blk, valid, target_pot, row_blocks):
    width = tiles.shape[-1]
    pieces = target_pot.reshape(-1, width)[cols_blk]
    score = pieces[:, None, :] - tiles.astype(jnp.float32)
    slot_top = jnp.max(score, axis=2)

    def row_summed(own_top):
        return jnp.sum(jnp.exp(score - own_top[:, :, None]), axis=2)

    return block_reduce(slot_top, row_summed, rows_blk, row_blocks, valid)


def col_partial(tiles, rows_blk, cols_blk, valid, source_pot, col_blocks):
    width = tiles.shape[-1]
    pieces = source_pot.reshape(-1, width)[rows_blk]
    score = pieces[:, :, None] - tiles.astype(jnp.float32)
    slot_top = jnp.max(score, axis=1)

    def col_summed(own_top):
        return jnp.sum(jnp.exp(score - own_top[:, None, :]), axis=1)

    return block_reduce(slot_top, col_summed, cols_blk, col_blocks, valid)


def per_device(costs, block_rows, block_cols, live, log_source, log_target):
    tiles = costs[0, 0]
    rows_blk = block_rows[0, 0]
    cols_blk = block_cols[0, 0]
    count = live[0, 0]
    width = tiles.shape[-1]
    valid = jnp.arange(tiles.shape[0], dtype=jnp.int32) < count
    src_len = log_source.shape[0]
    tgt_len = log_target.shape[0]
    row_blocks = src_len // width
    col_blocks = tgt_len // width
    target_pot = jnp.zeros((tgt_len,), jnp.float32)
    source_pot = jnp.zeros((src_len,), jnp.float32)
    for sweep in range(ITERS):
        top, total = row_partial(tiles, rows_blk, cols_blk, valid, target_pot, row_blocks)
        common = lax.pmax(top, "cols")
        total = lax.psum(total * jnp.exp(top - common), "cols")
        top = common
        source_pot = log_source - (top + jnp.log(total))
        col_top, col_tot = col_partial(tiles, rows_blk, cols_blk, valid, source_pot, col_blocks)
        col_top, col_tot = combined_all((col_top, col_tot), "rows", combine)
        target_pot = log_target - (col_top + jnp.log(col_tot))
    return (source_pot, target_pot)


def solution(mesh):
    in_specs = (
        P("rows", "cols", None, None, None),
        P("rows", "cols", None),
        P("rows", "cols", None),
        P("rows", "cols"),
        P("rows"),
        P("cols"),
    )
    out_specs = (P("rows"), P("cols"))
    return jax.shard_map(
        per_device, mesh=mesh, in_specs=in_specs, out_specs=out_specs, check_vma=False
    )
```

profile of v0, /device:TPU:0, one launch (start us, length us, event | category | flops | bytes accessed | tf_op | source)
XLA Modules:
  0.0 195.3 jit_solution(16827550042038354003)
XLA Ops:
  1.4 0.9 fusion.24
  2.3 0.7 fusion.26
  3.0 0.6 gather_fusion
  3.6 2.8 %fusion.1 = f32[24,256]{1,0:T(8,128)S(1)} fusion(bf16[1,1,24,256,256]{4,3,2,1,0:T(8,128)(2,1)} %param.12, f32[24,256]{1,0:T(8,128)S(1)} %gather_fusion), kind=kLoop, calls=%fused_computation.22 | loop fusion | flops 4712448 | bytes 3194880 | tf_op jit(solution)/shard_map/reduce_max | solution.py:42
  6.7 2.1 %fusion.23 = f32[24,256]{1,0:T(8,128)S(1)} fusion(bf16[1,1,24,256,256]{4,3,2,1,0:T(8,128)(2,1)S(1)} %copy-done, f32[24,256]{1,0:T(8,128)S(1)} %broadcast_select_fusion.11, f32[24,256]{1,0:T(8,128)S(1)} %gather_fusion), kind=kLoop, calls=%fused_computation.44 | loop fusion | flops 6285312 | bytes 3219456 | tf_op jit(solution)/shard_map/reduce_sum | solution.py:45
  9.0 23.4 %pmax.21 = f32[2048]{0:T(1024)S(1)} all-reduce(f32[2048]{0:T(1024)S(1)} %bitcast.98), channel_id=1, replica_groups=mesh['rows'=4,'cols'=8] {'cols'}, use_global_device_ids=true, to_apply=%region_2.3 | all-reduce | flops 2048 | bytes 16384 | tf_op jit(solution)/shard_map/pmax | solution.py:77
  32.4 17.4 %psum.21 = f32[2048]{0:T(1024)S(1)} all-reduce(f32[2048]{0:T(1024)S(1)} %exponential_multiply_fusion.2), channel_id=1, replica_groups=mesh['rows'=4,'cols'=8] {'cols'}, use_global_device_ids=true, to_apply=%region_6.7 | all-reduce | flops 2048 | bytes 16384 | tf_op jit(solution)/shard_map/psum | solution.py:78
  49.9 0.6 gather_fusion.1
  50.5 1.0 fusion.3
  52.4 1.6 fusion.21
  54.4 5.8 %all-gather.1 = f32[4,1,16384]{2,1,0:T(1,128)S(1)} all-gather(f32[1,1,16384]{2,1,0:T(1,128)S(1)} %reshape.438), channel_id=1, replica_groups=mesh['rows'=4,'cols'=8] {'rows'}, dimensions={0}, use_global_device_ids=true | all-gather | bytes 327680 | tf_op jit(solution)/shard_map/all_gather | solution.py:11
  60.4 0.7 reshape.436
  61.0 6.0 %all-gather = f32[4,1,16384]{2,1,0:T(1,128)S(1)} all-gather(f32[1,1,16384]{2,1,0:T(1,128)} %reshape.436), channel_id=1, replica_groups=mesh['rows'=4,'cols'=8] {'rows'}, dimensions={0}, use_global_device_ids=true | all-gather | bytes 327680 | tf_op jit(solution)/shard_map/all_gather | solution.py:11
  67.1 0.9 copy.31
  68.0 3.6 %while.51 = (s32[]{:T(128)}, f32[16384]{0:T(1024)S(1)}, f32[16384]{0:T(1024)S(1)}, f32[4,16384]{1,0:T(4,128)}, f32[4,16384]{1,0:T(4,128)S(1)}, /*index=5*/s32[]{:T(128)}, s32[]{:T(128)}, s32[]{:T(128)}) while((s32[]{:T(128)}, f32[16384]{0:T(1024)S(1)}, f32[16384]{0:T(1024)S(1)}, f32[4,16384]{1,0:T(4,128)}, f32[4,16384]{1,0:T(4,128)S(1)}, ...), condition=%wide.region_13.14_spmd, body=%wide.region_12.13_spmd.sunk | while | flops 98309 | bytes 655491 | solution.py:17
  68.0 1.1 constant_dynamic-slice_fusion.9
  69.2 1.1 constant_dynamic-slice_fusion.9
  70.4 1.1 constant_dynamic-slice_fusion.9
  71.6 0.9 add_subtract_fusion.2
  72.5 0.6 gather_fusion.2
  73.1 1.0 fusion.5
  74.4 2.1 %fusion.19 = f32[24,256]{1,0:T(8,128)S(1)} fusion(bf16[1,1,24,256,256]{4,3,2,1,0:T(8,128)(2,1)S(1)} %copy-done, f32[24,256]{1,0:T(8,128)S(1)} %broadcast_select_fusion.7, f32[24,256]{1,0:T(8,128)S(1)} %gather_fusion.2), kind=kLoop, calls=%fused_computation.40 | loop fusion | flops 6285312 | bytes 3219456 | tf_op jit(solution)/shard_map/reduce_sum | solution.py:45
  76.7 19.4 %pmax.22 = f32[2048]{0:T(1024)S(1)} all-reduce(f32[2048]{0:T(1024)S(1)} %bitcast.100), channel_id=1, replica_groups=mesh['rows'=4,'cols'=8] {'cols'}, use_global_device_ids=true, to_apply=%region_16.17 | all-reduce | flops 2048 | bytes 16384 | tf_op jit(solution)/shard_map/pmax | solution.py:77
  96.1 17.4 %psum.22 = f32[2048]{0:T(1024)S(1)} all-reduce(f32[2048]{0:T(1024)S(1)} %exponential_multiply_fusion.1), channel_id=1, replica_groups=mesh['rows'=4,'cols'=8] {'cols'}, use_global_device_ids=true, to_apply=%region_20.21 | all-reduce | flops 2048 | bytes 16384 | tf_op jit(solution)/shard_map/psum | solution.py:78
  113.5 0.7 gather_fusion.3
  114.2 1.0 fusion.7
  116.0 1.6 fusion.17
  118.0 5.8 %all-gather.3 = f32[4,1,16384]{2,1,0:T(1,128)S(1)} all-gather(f32[1,1,16384]{2,1,0:T(1,128)S(1)} %reshape.442), channel_id=1, replica_groups=mesh['rows'=4,'cols'=8] {'rows'}, dimensions={0}, use_global_device_ids=true | all-gather | bytes 327680 | tf_op jit(solution)/shard_map/all_gather | solution.py:11
  124.0 0.7 reshape.440
  124.7 6.2 %all-gather.2 = f32[4,1,16384]{2,1,0:T(1,128)S(1)} all-gather(f32[1,1,16384]{2,1,0:T(1,128)} %reshape.440), channel_id=1, replica_groups=mesh['rows'=4,'cols'=8] {'rows'}, dimensions={0}, use_global_device_ids=true | all-gather | bytes 327680 | tf_op jit(solution)/shard_map/all_gather | solution.py:11
  130.9 0.9 copy.29
  131.8 3.6 %while.52 = (s32[]{:T(128)}, f32[16384]{0:T(1024)S(1)}, f32[16384]{0:T(1024)S(1)}, f32[4,16384]{1,0:T(4,128)}, f32[4,16384]{1,0:T(4,128)S(1)}, /*index=5*/s32[]{:T(128)}, s32[]{:T(128)}, s32[]{:T(128)}) while((s32[]{:T(128)}, f32[16384]{0:T(1024)S(1)}, f32[16384]{0:T(1024)S(1)}, f32[4,16384]{1,0:T(4,128)}, f32[4,16384]{1,0:T(4,128)S(1)}, ...), condition=%wide.region_27.28_spmd, body=%wide.region_26.27_spmd.sunk | while | flops 98309 | bytes 655491 | solution.py:17
  131.8 1.1 constant_dynamic-slice_fusion.10
  132.9 1.1 constant_dynamic-slice_fusion.10
  134.2 1.1 constant_dynamic-slice_fusion.10
  135.3 0.9 add_subtract_fusion.1
  136.2 0.6 gather_fusion.4
  136.8 1.0 fusion.9
  138.2 2.1 %fusion.15 = f32[24,256]{1,0:T(8,128)S(1)} fusion(bf16[1,1,24,256,256]{4,3,2,1,0:T(8,128)(2,1)S(1)} %copy-done, f32[24,256]{1,0:T(8,128)S(1)} %broadcast_select_fusion.3, f32[24,256]{1,0:T(8,128)S(1)} %gather_fusion.4), kind=kLoop, calls=%fused_computation.36 | loop fusion | flops 6285312 | bytes 3219456 | tf_op jit(solution)/shard_map/reduce_sum | solution.py:45
  140.4 19.4 %pmax.23 = f32[2048]{0:T(1024)S(1)} all-reduce(f32[2048]{0:T(1024)S(1)} %bitcast.102), channel_id=1, replica_groups=mesh['rows'=4,'cols'=8] {'cols'}, use_global_device_ids=true, to_apply=%region_30.31 | all-reduce | flops 2048 | bytes 16384 | tf_op jit(solution)/shard_map/pmax | solution.py:77
  159.9 17.4 %psum.23 = f32[2048]{0:T(1024)S(1)} all-reduce(f32[2048]{0:T(1024)S(1)} %exponential_multiply_fusion), channel_id=1, replica_groups=mesh['rows'=4,'cols'=8] {'cols'}, use_global_device_ids=true, to_apply=%region_34.35 | all-reduce | flops 2048 | bytes 16384 | tf_op jit(solution)/shard_map/psum | solution.py:78
  177.3 0.7 gather_fusion.5
  178.0 1.0 fusion.11
  179.8 1.6 fusion.13
  181.8 5.8 %all-gather.5 = f32[4,1,16384]{2,1,0:T(1,128)S(1)} all-gather(f32[1,1,16384]{2,1,0:T(1,128)S(1)} %reshape.446), channel_id=1, replica_groups=mesh['rows'=4,'cols'=8] {'rows'}, dimensions={0}, use_global_device_ids=true | all-gather | bytes 327680 | tf_op jit(solution)/shard_map/all_gather | solution.py:11
  187.9 5.9 %all-gather.4 = f32[4,1,16384]{2,1,0:T(1,128)S(1)} all-gather(f32[1,1,16384]{2,1,0:T(1,128)S(1)} %reshape.444), channel_id=1, replica_groups=mesh['rows'=4,'cols'=8] {'rows'}, dimensions={0}, use_global_device_ids=true | all-gather | bytes 327680 | tf_op jit(solution)/shard_map/all_gather | solution.py:11
  193.9 0.7 while.53
  194.6 0.6 add_subtract_fusion
  (97 shorter events, 6.8 us)
Async XLA Ops:
  0.6 6.1 %copy-start = (bf16[1,1,24,256,256]{4,3,2,1,0:T(8,128)(2,1)S(1)}, bf16[1,1,24,256,256]{4,3,2,1,0:T(8,128)(2,1)}, u32[]{:S(2)}) copy-start(bf16[1,1,24,256,256]{4,3,2,1,0:T(8,128)(2,1)} %param.12) | copy-start | bytes 9437188
  3.6 46.2 %copy-start.2 = (f32[2048]{0:T(1024)S(1)}, f32[2048]{0:T(1024)}, u32[]{:S(2)}) copy-start(f32[2048]{0:T(1024)} %param.16) | copy-start | bytes 24580
  3.6 46.3 %copy-start.7 = (s32[1,1,24]{2,1,0:T(1,128)S(1)}, s32[1,1,24]{2,1,0:T(1,128)}, u32[]{:S(2)}) copy-start(s32[1,1,24]{2,1,0:T(1,128)} %param.13) | copy-start | bytes 292
  6.7 44.8 %copy-start.8 = (s32[1,1,24]{2,1,0:T(1,128)S(1)}, s32[1,1,24]{2,1,0:T(1,128)}, u32[]{:S(2)}) copy-start(s32[1,1,24]{2,1,0:T(1,128)} %param.14) | copy-start | bytes 292
  49.9 1.7 copy-start.6
  73.0 40.4 %copy-start.3 = (f32[2048]{0:T(1024)S(1)}, f32[2048]{0:T(1024)}, u32[]{:S(2)}) copy-start(f32[2048]{0:T(1024)} %param.16) | copy-start | bytes 24580
  136.8 40.4 %copy-start.4 = (f32[2048]{0:T(1024)S(1)}, f32[2048]{0:T(1024)}, u32[]{:S(2)}) copy-start(f32[2048]{0:T(1024)} %param.16) | copy-start | bytes 24580
  177.3 4.1 %copy-start.5 = (f32[2048]{0:T(1024)}, f32[2048]{0:T(1024)S(1)}, u32[]{:S(2)}) copy-start(f32[2048]{0:T(1024)S(1)} %add_subtract_fusion.3) | copy-start | bytes 24580
  181.4 13.2 %copy-start.1 = (f32[16384]{0:T(1024)S(1)}, f32[16384]{0:T(1024)}, u32[]{:S(2)}) copy-start(f32[16384]{0:T(1024)} %param.17) | copy-start | bytes 196612
where the time goes:
time: 196 us; the launch traced here: 195 us
  blocking collectives  150 us (77%)
  other arithmetic  28.1 us (14%)
  local copies, waits for them, and re-layouts  15.1 us (8%)
  between operations  2.1 us (1%)
    pmax x3, blocking collectives, per_device(): common = lax.pmax(top, 'cols')  62.2 us
    psum x3, blocking collectives, per_device(): total = lax.psum(total * jnp.exp(top - common), 'cols')  52.1 us
    all_gather x6, blocking collectives, combined_all(): everything = jax.tree.map(lambda part: lax.all_gather(part, axis), value)  35.5 us
    dynamic_slice x9, local copies, waits for them, and re-layouts, hop(): return combine(so_far, jax.tree.map(lambda part: part[k], everything))  7.07 us
    reduce_sum x3, other arithmetic, row_summed(): return jnp.sum(jnp.exp(score - own_top[:, :, None]), axis=2)  6.26 us
    reduce_sum x3, other arithmetic, col_summed(): return jnp.sum(jnp.exp(score - own_top[:, None, :]), axis=1)  4.79 us
    reduce_max x3, other arithmetic, row_partial(): slot_top = jnp.max(score, axis=2)  4.78 us
    unnamed x36, local copies, waits for them, and re-layouts  4.16 us

commit v1 on v0

--- a/solution.py
+++ b/solution.py
@@ -75,7 +75,7 @@
     for sweep in range(ITERS):
         top, total = row_partial(tiles, rows_blk, cols_blk, valid, target_pot, row_blocks)
         common = lax.pmax(top, "cols")
-        total = lax.psum(total * jnp.exp(top - common), "cols")
+        total = jnp.sum(lax.all_gather(total * jnp.exp(top - common), "cols"), axis=0)
         top = common
         source_pot = log_source - (top + jnp.log(total))
         col_top, col_tot = col_partial(tiles, rows_blk, cols_blk, valid, source_pot, col_blocks)

time: 196 us -> 233 us (1.19)
  blocking collectives: 150 us -> 187 us
    all_gather x0 -> x3, blocking collectives: none -> 91.6 us  [per_device(): lax.all_gather(total * jnp.exp(top - common), 'cols')]
    psum x3 -> x0, blocking collectives: 52.1 us -> none  [per_device(): total = lax.psum(total * jnp.exp(top - common), 'cols')]
where the time goes in v1:
time: 233 us
  blocking collectives  187 us (80%)
  other arithmetic  28.2 us (12%)
  local copies, waits for them, and re-layouts  15.2 us (7%)
    all_gather x3, blocking collectives, per_device(): lax.all_gather(total * jnp.exp(top - common), 'cols')  91.6 us
    pmax x3, blocking collectives, per_device(): common = lax.pmax(top, 'cols')  60.2 us
    all_gather x6, blocking collectives, combined_all(): everything = jax.tree.map(lambda part: lax.all_gather(part, axis), value)  35.5 us
    dynamic_slice x9, local copies, waits for them, and re-layouts, hop(): return combine(so_far, jax.tree.map(lambda part: part[k], everything))  7.07 us
    reduce_sum x3, other arithmetic, row_summed(): return jnp.sum(jnp.exp(score - own_top[:, :, None]), axis=2)  6.26 us
    reduce_sum x3, other arithmetic, col_summed(): return jnp.sum(jnp.exp(score - own_top[:, None, :]), axis=1)  4.79 us
    reduce_max x3, other arithmetic, row_partial(): slot_top = jnp.max(score, axis=2)  4.78 us

profile of v1, /device:TPU:0, one launch (start us, length us, event | category | flops | bytes accessed | tf_op | source)
XLA Modules:
  0.0 232.9 jit_solution(17026967554196938582)
XLA Ops:
  1.4 0.9 fusion.24
  2.3 0.7 fusion.26
  3.0 0.6 gather_fusion
  3.6 2.8 %fusion.1 = f32[24,256]{1,0:T(8,128)S(1)} fusion(bf16[1,1,24,256,256]{4,3,2,1,0:T(8,128)(2,1)} %param.12, f32[24,256]{1,0:T(8,128)S(1)} %gather_fusion), kind=kLoop, calls=%fused_computation.22 | loop fusion | flops 4712448 | bytes 3194880 | tf_op jit(solution)/shard_map/reduce_max | solution.py:42
  6.7 2.1 fusion.23
  9.0 23.4 %pmax.21 = f32[2048]{0:T(1024)S(1)} all-reduce(f32[2048]{0:T(1024)S(1)} %bitcast.98), channel_id=1, replica_groups=mesh['rows'=4,'cols'=8] {'cols'}, use_global_device_ids=true, to_apply=%region_2.3 | all-reduce | flops 2048 | bytes 16384 | tf_op jit(solution)/shard_map/pmax | solution.py:77
  32.4 30.5 %all-gather = f32[16384]{0:T(1024)S(1)} all-gather(f32[2048]{0:T(1024)S(1)} %exponential_multiply_fusion.2), channel_id=2, replica_groups=mesh['rows'=4,'cols'=8] {'cols'}, dimensions={0}, use_global_device_ids=true | all-gather | bytes 73728 | tf_op jit(solution)/shard_map/all_gather | solution.py:78
  63.1 0.6 gather_fusion.1
  63.7 1.0 fusion.3
  65.6 1.6 fusion.21
  67.6 5.8 %all-gather.4 = f32[4,1,16384]{2,1,0:T(1,128)S(1)} all-gather(f32[1,1,16384]{2,1,0:T(1,128)S(1)} %reshape.441), channel_id=1, replica_groups=mesh['rows'=4,'cols'=8] {'rows'}, dimensions={0}, use_global_device_ids=true | all-gather | bytes 327680 | tf_op jit(solution)/shard_map/all_gather | solution.py:11
  73.5 0.7 reshape.439
  74.2 6.0 %all-gather.3 = f32[4,1,16384]{2,1,0:T(1,128)S(1)} all-gather(f32[1,1,16384]{2,1,0:T(1,128)} %reshape.439), channel_id=1, replica_groups=mesh['rows'=4,'cols'=8] {'rows'}, dimensions={0}, use_global_device_ids=true | all-gather | bytes 327680 | tf_op jit(solution)/shard_map/all_gather | solution.py:11
  80.3 0.9 copy.31
  81.2 3.6 %while.51 = (s32[]{:T(128)}, f32[16384]{0:T(1024)S(1)}, f32[16384]{0:T(1024)S(1)}, f32[4,16384]{1,0:T(4,128)}, f32[4,16384]{1,0:T(4,128)S(1)}, /*index=5*/s32[]{:T(128)}, s32[]{:T(128)}, s32[]{:T(128)}) while((s32[]{:T(128)}, f32[16384]{0:T(1024)S(1)}, f32[16384]{0:T(1024)S(1)}, f32[4,16384]{1,0:T(4,128)}, f32[4,16384]{1,0:T(4,128)S(1)}, ...), condition=%wide.region_13.14_spmd, body=%wide.region_12.13_spmd.sunk | while | flops 98309 | bytes 655491 | solution.py:17
  81.2 1.1 constant_dynamic-slice_fusion.9
  82.4 1.1 constant_dynamic-slice_fusion.9
  83.6 1.1 constant_dynamic-slice_fusion.9
  84.8 0.9 add_subtract_fusion.2
  85.7 0.6 gather_fusion.2
  86.3 1.0 fusion.5
  87.6 2.1 fusion.19
  89.9 17.4 %pmax.22 = f32[2048]{0:T(1024)S(1)} all-reduce(f32[2048]{0:T(1024)S(1)} %bitcast.100), channel_id=1, replica_groups=mesh['rows'=4,'cols'=8] {'cols'}, use_global_device_ids=true, to_apply=%region_16.17 | all-reduce | flops 2048 | bytes 16384 | tf_op jit(solution)/shard_map/pmax | solution.py:77
  107.3 30.5 %all-gather.1 = f32[16384]{0:T(1024)S(1)} all-gather(f32[2048]{0:T(1024)S(1)} %exponential_multiply_fusion.1), channel_id=3, replica_groups=mesh['rows'=4,'cols'=8] {'cols'}, dimensions={0}, use_global_device_ids=true | all-gather | bytes 73728 | tf_op jit(solution)/shard_map/all_gather | solution.py:78
  137.9 0.7 gather_fusion.3
  138.6 1.0 fusion.7
  140.4 1.6 fusion.17
  142.4 5.8 %all-gather.6 = f32[4,1,16384]{2,1,0:T(1,128)S(1)} all-gather(f32[1,1,16384]{2,1,0:T(1,128)S(1)} %reshape.445), channel_id=1, replica_groups=mesh['rows'=4,'cols'=8] {'rows'}, dimensions={0}, use_global_device_ids=true | all-gather | bytes 327680 | tf_op jit(solution)/shard_map/all_gather | solution.py:11
  148.3 0.7 reshape.443
  149.0 6.2 %all-gather.5 = f32[4,1,16384]{2,1,0:T(1,128)S(1)} all-gather(f32[1,1,16384]{2,1,0:T(1,128)} %reshape.443), channel_id=1, replica_groups=mesh['rows'=4,'cols'=8] {'rows'}, dimensions={0}, use_global_device_ids=true | all-gather | bytes 327680 | tf_op jit(solution)/shard_map/all_gather | solution.py:11
  155.3 0.9 copy.29
  156.1 3.6 %while.52 = (s32[]{:T(128)}, f32[16384]{0:T(1024)S(1)}, f32[16384]{0:T(1024)S(1)}, f32[4,16384]{1,0:T(4,128)}, f32[4,16384]{1,0:T(4,128)S(1)}, /*index=5*/s32[]{:T(128)}, s32[]{:T(128)}, s32[]{:T(128)}) while((s32[]{:T(128)}, f32[16384]{0:T(1024)S(1)}, f32[16384]{0:T(1024)S(1)}, f32[4,16384]{1,0:T(4,128)}, f32[4,16384]{1,0:T(4,128)S(1)}, ...), condition=%wide.region_27.28_spmd, body=%wide.region_26.27_spmd.sunk | while | flops 98309 | bytes 655491 | solution.py:17
  156.1 1.1 constant_dynamic-slice_fusion.10
  157.3 1.1 constant_dynamic-slice_fusion.10
  158.5 1.1 constant_dynamic-slice_fusion.10
  159.7 0.9 add_subtract_fusion.1
  160.6 0.6 gather_fusion.4
  161.2 1.0 fusion.9
  162.5 2.1 fusion.15
  164.8 19.4 %pmax.23 = f32[2048]{0:T(1024)S(1)} all-reduce(f32[2048]{0:T(1024)S(1)} %bitcast.102), channel_id=1, replica_groups=mesh['rows'=4,'cols'=8] {'cols'}, use_global_device_ids=true, to_apply=%region_30.31 | all-reduce | flops 2048 | bytes 16384 | tf_op jit(solution)/shard_map/pmax | solution.py:77
  184.3 30.5 %all-gather.2 = f32[16384]{0:T(1024)S(1)} all-gather(f32[2048]{0:T(1024)S(1)} %exponential_multiply_fusion), channel_id=4, replica_groups=mesh['rows'=4,'cols'=8] {'cols'}, dimensions={0}, use_global_device_ids=true | all-gather | bytes 73728 | tf_op jit(solution)/shard_map/all_gather | solution.py:78
  214.9 0.7 gather_fusion.5
  215.6 1.0 fusion.11
  217.4 1.6 fusion.13
  219.4 5.8 %all-gather.8 = f32[4,1,16384]{2,1,0:T(1,128)S(1)} all-gather(f32[1,1,16384]{2,1,0:T(1,128)S(1)} %reshape.449), channel_id=1, replica_groups=mesh['rows'=4,'cols'=8] {'rows'}, dimensions={0}, use_global_device_ids=true | all-gather | bytes 327680 | tf_op jit(solution)/shard_map/all_gather | solution.py:11
  225.5 5.9 %all-gather.7 = f32[4,1,16384]{2,1,0:T(1,128)S(1)} all-gather(f32[1,1,16384]{2,1,0:T(1,128)S(1)} %reshape.447), channel_id=1, replica_groups=mesh['rows'=4,'cols'=8] {'rows'}, dimensions={0}, use_global_device_ids=true | all-gather | bytes 327680 | tf_op jit(solution)/shard_map/all_gather | solution.py:11
  231.5 0.7 while.53
  232.2 0.6 add_subtract_fusion
  (103 shorter events, 6.9 us)
Async XLA Ops:
  0.6 6.1 %copy-start = (bf16[1,1,24,256,256]{4,3,2,1,0:T(8,128)(2,1)S(1)}, bf16[1,1,24,256,256]{4,3,2,1,0:T(8,128)(2,1)}, u32[]{:S(2)}) copy-start(bf16[1,1,24,256,256]{4,3,2,1,0:T(8,128)(2,1)} %param.12) | copy-start | bytes 9437188
  3.6 59.4 %copy-start.2 = (f32[2048]{0:T(1024)S(1)}, f32[2048]{0:T(1024)}, u32[]{:S(2)}) copy-start(f32[2048]{0:T(1024)} %param.16) | copy-start | bytes 24580
  3.6 59.5 %copy-start.7 = (s32[1,1,24]{2,1,0:T(1,128)S(1)}, s32[1,1,24]{2,1,0:T(1,128)}, u32[]{:S(2)}) copy-start(s32[1,1,24]{2,1,0:T(1,128)} %param.13) | copy-start | bytes 292
  6.7 58.0 %copy-start.8 = (s32[1,1,24]{2,1,0:T(1,128)S(1)}, s32[1,1,24]{2,1,0:T(1,128)}, u32[]{:S(2)}) copy-start(s32[1,1,24]{2,1,0:T(1,128)} %param.14) | copy-start | bytes 292
  63.1 1.7 copy-start.6
  86.2 51.6 %copy-start.3 = (f32[2048]{0:T(1024)S(1)}, f32[2048]{0:T(1024)}, u32[]{:S(2)}) copy-start(f32[2048]{0:T(1024)} %param.16) | copy-start | bytes 24580
  161.2 53.6 %copy-start.4 = (f32[2048]{0:T(1024)S(1)}, f32[2048]{0:T(1024)}, u32[]{:S(2)}) copy-start(f32[2048]{0:T(1024)} %param.16) | copy-start | bytes 24580
  214.9 4.1 %copy-start.5 = (f32[2048]{0:T(1024)}, f32[2048]{0:T(1024)S(1)}, u32[]{:S(2)}) copy-start(f32[2048]{0:T(1024)S(1)} %add_subtract_fusion.3) | copy-start | bytes 24580
  219.0 13.2 %copy-start.1 = (f32[16384]{0:T(1024)S(1)}, f32[16384]{0:T(1024)}, u32[]{:S(2)}) copy-start(f32[16384]{0:T(1024)} %param.17) | copy-start | bytes 196612
